TPU v7x, 256 devices: a whole 4x4x8 slice. The times are simulated.
256 devices in a mesh: tm: 8 (over z_hi, x), space: 32 (over y, z_lo, core).
Axes of the slice: x: 4, y: 4, z: 8 (z_hi: 2, z_lo: 4; z = z_hi * 4 + z_lo), core: 2. Of those that a mesh axis runs over, the one named last changes fastest.
Arguments:
- eof_basis: bfloat16 [262144, 256], P('space'), may hold values from -0.01171875 to 0.01171875
- snapshots: bfloat16 [262144, 512], P('space', 'tm'), may hold values from -6 to 6
- inverse_energy: float32 [256], replicated, may hold values from 0.022097087 to 0.22097087
- eigen_vectors: bfloat16 [256, 512], replicated, may hold values from -0.375 to 0.375
Outputs:
- reduced_operator: float32 [256, 256], replicated
- rebuilt_modes: bfloat16 [512, 262144], P('tm', 'space')
All inputs are finite; a program needn't handle non-finite values.
Results may differ from a plain program's by a relative error of at most 0.0049.
Values may be sent and summed in bfloat16 or wider, within the bound.
A program may use at most 64 MiB of HBM per device.

v0:
```python
import jax
import jax.numpy as jnp
from jax import lax
from jax.sharding import PartitionSpec as P


def passed_along(block, axis, distance):
    devices = range(lax.axis_size(axis))
    route = [(i - distance, i) for i in devices if i - distance in devices]
    return lax.ppermute(block, axis, route)


def per_device(eof_basis, snapshots, inverse_energy, eigen_vectors):
    partial_value = lax.dot_general(
        eof_basis, snapshots, (((0,), (0,)), ((), ())), preferred_element_type=jnp.float32
    )
    coeffs = lax.psum(partial_value, "space")
    previous = passed_along(coeffs[:, -1:], "tm", 1)
    lagged = jnp.concatenate([previous, coeffs[:, :-1]], axis=1)
    scaled = lagged * inverse_energy[:, None]
    local_part = jnp.dot(coeffs, scaled.T, precision=lax.Precision.HIGHEST)
    reduced_operator = lax.psum(local_part, "tm")
    hour_weights = jnp.dot(
        scaled.T, eigen_vectors.astype(jnp.float32), precision=lax.Precision.HIGHEST
    ).astype(jnp.bfloat16)
    rebuilt = lax.psum_scatter(
        lax.dot_general(
            hour_weights, snapshots, (((0,), (1,)), ((), ())), preferred_element_type=jnp.float32
        ),
        "tm",
        scatter_dimension=0,
        tiled=True,
    )
    return (reduced_operator, rebuilt.astype(jnp.bfloat16))


def solution(mesh):
    in_specs = (P("space", None), P("space", "tm"), P(), P())
    out_specs = (P(), P("tm", "space"))
    return jax.shard_map(
        per_device, mesh=mesh, in_specs=in_specs, out_specs=out_specs, check_vma=False
    )
```

profile of v0, /device:TPU:8, one launch (start us, length us, event | category | flops | bytes accessed | tf_op | source)
XLA Modules:
  0.0 729.5 jit_solution(18432330371849172905)
XLA Ops:
  7.2 0.0 copy-start
  7.2 0.0 copy-start.3
  7.2 0.0 copy-start.2
  7.2 0.0 all-reduce.3.cloned.1.call-start
  7.2 1.1 copy-done
  8.4 3.6 fusion.6
  12.0 0.0 all-reduce.3.cloned.1.call-update
  12.0 0.0 reduce-scatter.2.cloned.1.call-start
  12.1 231.5 %all-reduce.3.cloned.1.call-done = f32[256,64]{0,1:T(8,128)} async-done(((f32[256,64]{0,1:T(8,128)}), f32[256,64]{0,1:T(8,128)}) %all-reduce.3.cloned.1.call-update) | async-done | bytes 65552 | tf_op jit(solution)/shard_map/psum | solution.py:17
  243.6 0.7 slice.8
  244.3 3.4 collective-permute-start
  247.7 1.3 collective-permute-done
  249.0 0.0 copy-done.3
  249.0 0.0 copy-done.2
  249.0 1.1 convolution_convert_fusion
  250.1 8.1 %fusion.5 = f32[512,8192]{1,0:T(8,128)} fusion(bf16[64,512]{1,0:T(8,128)(2,1)S(1)} %convolution_convert_fusion, bf16[8192,64]{0,1:T(8,128)(2,1)S(1)} %copy-done), kind=kOutput, calls=%fused_computation.7 | convolution fusion | flops 536870912 | bytes 17891328 | tf_op jit(solution)/shard_map/dot_general | solution.py:27
  258.2 0.0 copy-start.1
  258.2 0.0 reduce-scatter.2.cloned.1.call-update
  258.2 0.0 all-reduce.5.cloned.1.call-start
  258.2 0.8 copy-done.1
  259.0 1.1 fusion
  260.1 0.0 all-reduce.5.cloned.1.call-update
  260.2 339.3 %reduce-scatter.2.cloned.1.call-done = f32[64,8192]{1,0:T(8,128)} async-done(((f32[512,8192]{1,0:T(8,128)}), f32[64,8192]{1,0:T(8,128)}) %reduce-scatter.2.cloned.1.call-update) | async-done | bytes 2097168 | tf_op jit(solution)/shard_map/reduce_scatter | solution.py:26
  599.5 2.7 convert_element_type.8
  602.1 119.2 %all-reduce.5.cloned.1.call-done = f32[256,256]{1,0:T(8,128)} async-done(((f32[256,256]{1,0:T(8,128)}), f32[256,256]{1,0:T(8,128)}) %all-reduce.5.cloned.1.call-update) | async-done | bytes 262160 | tf_op jit(solution)/shard_map/psum | solution.py:22
  721.3 1.7 copy.8
Async XLA Ops:
  7.2 1.2 copy-start
  7.2 241.8 %copy-start.3 = (f32[256]{0:T(256)S(1)}, f32[256]{0:T(256)}, u32[]{:S(2)}) copy-start(f32[256]{0:T(256)} %param.6) | copy-start | bytes 3076
  7.2 241.8 %copy-start.2 = (bf16[256,512]{1,0:T(8,128)(2,1)S(1)}, bf16[256,512]{1,0:T(8,128)(2,1)}, u32[]{:S(2)}) copy-start(bf16[256,512]{1,0:T(8,128)(2,1)} %param.7) | copy-start | bytes 786436
  7.2 236.4 %all-reduce.3.cloned.1.call-start = ((), (), s32[]{:S(2)}) async-start(), calls=%async_computation.1 | async-start | bytes 131072 | tf_op jit(solution)/shard_map/psum | solution.py:17
  12.0 587.4 %reduce-scatter.2.cloned.1.call-start = ((), (), s32[]{:S(2)}) async-start(), calls=%async_computation.3 | async-start | bytes 18874368 | tf_op jit(solution)/shard_map/reduce_scatter | solution.py:26
  244.3 4.7 collective-permute-start
  258.2 0.8 copy-start.1
  258.2 463.1 %all-reduce.5.cloned.1.call-start = ((), (), s32[]{:S(2)}) async-start(), calls=%async_computation.2 | async-start | bytes 524288 | tf_op jit(solution)/shard_map/psum | solution.py:22
Sparse Core Ops, SparseCore 0:
  12.2 231.4 all-reduce.2
  258.3 341.0 reduce-scatter.1
  602.7 118.6 all-reduce.4
where the time goes:
time: 730 us
  waiting for transfers between devices  691 us (95%)
  matrix products  13.9 us (2%)
  between operations  13.8 us (2%)
    reduce_scatter x1, waiting for transfers between devices, per_device(): lax.psum_scatter(lax.dot_general(hour_weights, snapshots, (((0,), (1,)),...  339 us
    psum x1, waiting for transfers between devices, per_device(): coeffs = lax.psum(partial_value, 'space')  232 us
    psum x1, waiting for transfers between devices, per_device(): reduced_operator = lax.psum(local_part, 'tm')  119 us
  transfers between devices with their start and end apart: 4, of which 4 were waited for; matrix products, arithmetic and copies ran while one was open for 1% of the time, Pallas kernels for 0%

commit v1 on v0

--- a/solution.py
+++ b/solution.py
@@ -1,7 +1,15 @@
+import functools
 import jax
 import jax.numpy as jnp
 from jax import lax
 from jax.sharding import PartitionSpec as P
+
+
+def carry_vector_now(piece_in, along_axis):
+    return lax.all_gather(piece_in, along_axis).sum(axis=0)
+
+
+produce_thing = functools.partial(carry_vector_now, along_axis="space")
 
 
 def passed_along(block, axis, distance):
@@ -14,7 +22,7 @@
     partial_value = lax.dot_general(
         eof_basis, snapshots, (((0,), (0,)), ((), ())), preferred_element_type=jnp.float32
     )
-    coeffs = lax.psum(partial_value, "space")
+    coeffs = produce_thing(partial_value)
     previous = passed_along(coeffs[:, -1:], "tm", 1)
     lagged = jnp.concatenate([previous, coeffs[:, :-1]], axis=1)
     scaled = lagged * inverse_energy[:, None]

time: 730 us -> 545 us (0.75)
  waiting for transfers between devices: 691 us -> 506 us
    psum x1 -> x0, waiting for transfers between devices: 232 us -> none  [per_device(): coeffs = lax.psum(partial_value, 'space')]
    all_gather x0 -> x1, waiting for transfers between devices: none -> 62.6 us  [carry_vector_now(): return lax.all_gather(piece_in, along_axis).sum(axis=0)]
    reduce_scatter x1, waiting for transfers between devices: 339 us -> 323 us  [per_device(): lax.psum_scatter(lax.dot_general(hour_weights, snapshots, (((0,), (1,)),...]
where the time goes in v1:
time: 545 us
  waiting for transfers between devices  506 us (93%)
  between operations  13.8 us (3%)
  matrix products  13.1 us (2%)
    reduce_scatter x1, waiting for transfers between devices, per_device(): lax.psum_scatter(lax.dot_general(hour_weights, snapshots, (((0,), (1,)),...  323 us
    psum x1, waiting for transfers between devices, per_device(): reduced_operator = lax.psum(local_part, 'tm')  119 us
    all_gather x1, waiting for transfers between devices, carry_vector_now(): return lax.all_gather(piece_in, along_axis).sum(axis=0)  62.6 us
  transfers between devices with their start and end apart: 4, of which 4 were waited for; matrix products, arithmetic and copies ran while one was open for 1% of the time, Pallas kernels for 0%

profile of v1, /device:TPU:8, one launch (start us, length us, event | category | flops | bytes accessed | tf_op | source)
XLA Modules:
  0.0 544.6 jit_solution(10341583326923322360)
XLA Ops:
  7.2 0.0 copy-start
  7.2 0.0 all-gather.3.cloned.1.call-start
  7.2 1.2 copy-done
  8.4 3.6 fusion.6
  12.0 0.0 copy-start.1
  12.0 0.0 copy-start.2
  12.0 0.0 all-gather.3.cloned.1.call-update
  12.0 0.0 reduce-scatter.2.cloned.1.call-start
  12.1 62.6 %all-gather.3.cloned.1.call-done = f32[8192,64]{0,1:T(8,128)} async-done(((f32[256,64]{0,1:T(8,128)}), f32[8192,64]{0,1:T(8,128)}) %all-gather.3.cloned.1.call-update) | async-done | bytes 2097168 | tf_op jit(solution)/shard_map/all_gather | solution.py:9
  74.6 2.2 copy.6
  76.9 0.2 bitcast_reduce_fusion
  77.1 3.4 collective-permute-start
  80.5 1.3 collective-permute-done
  81.8 0.0 copy-done.1
  81.8 0.0 copy-done.2
  81.8 0.3 convolution_convert_fusion
  82.0 8.1 %fusion.5 = f32[512,8192]{1,0:T(8,128)} fusion(bf16[64,512]{1,0:T(8,128)(2,1)S(1)} %convolution_convert_fusion, bf16[8192,64]{0,1:T(8,128)(2,1)S(1)} %copy-done), kind=kOutput, calls=%fused_computation.8 | convolution fusion | flops 536870912 | bytes 17891328 | tf_op jit(solution)/shard_map/dot_general | solution.py:35
  90.1 0.0 reduce-scatter.2.cloned.1.call-update
  90.2 0.0 all-reduce.2.cloned.1.call-start
  90.2 1.1 fusion
  91.3 0.0 all-reduce.2.cloned.1.call-update
  91.4 323.0 %reduce-scatter.2.cloned.1.call-done = f32[64,8192]{1,0:T(8,128)} async-done(((f32[512,8192]{1,0:T(8,128)}), f32[64,8192]{1,0:T(8,128)}) %reduce-scatter.2.cloned.1.call-update) | async-done | bytes 2097168 | tf_op jit(solution)/shard_map/reduce_scatter | solution.py:34
  414.4 2.7 convert_element_type.8
  417.1 119.4 %all-reduce.2.cloned.1.call-done = f32[256,256]{1,0:T(8,128)} async-done(((f32[256,256]{1,0:T(8,128)}), f32[256,256]{1,0:T(8,128)}) %all-reduce.2.cloned.1.call-update) | async-done | bytes 262160 | tf_op jit(solution)/shard_map/psum | solution.py:30
  536.4 1.7 copy.8
  (1 shorter events, 0.0 us)
Async XLA Ops:
  7.2 1.2 copy-start
  7.2 67.5 %all-gather.3.cloned.1.call-start = ((), (), s32[]{:S(2)}) async-start(), calls=%async_computation.3 | async-start | bytes 2162688 | tf_op jit(solution)/shard_map/all_gather | solution.py:9
  12.0 69.8 %copy-start.1 = (bf16[256,512]{1,0:T(8,128)(2,1)S(1)}, bf16[256,512]{1,0:T(8,128)(2,1)}, u32[]{:S(2)}) copy-start(bf16[256,512]{1,0:T(8,128)(2,1)} %param.7) | copy-start | bytes 786436
  12.0 69.8 %copy-start.2 = (f32[256]{0:T(256)S(1)}, f32[256]{0:T(256)}, u32[]{:S(2)}) copy-start(f32[256]{0:T(256)} %param.6) | copy-start | bytes 3076
  12.0 402.4 %reduce-scatter.2.cloned.1.call-start = ((), (), s32[]{:S(2)}) async-start(), calls=%async_computation.2 | async-start | bytes 18874368 | tf_op jit(solution)/shard_map/reduce_scatter | solution.py:34
  77.1 4.7 collective-permute-start
  90.2 446.3 %all-reduce.2.cloned.1.call-start = ((), (), s32[]{:S(2)}) async-start(), calls=%async_computation.1 | async-start | bytes 524288 | tf_op jit(solution)/shard_map/psum | solution.py:30
Sparse Core Ops, SparseCore 0:
  12.2 62.4 all-gather.2
  90.3 324.0 reduce-scatter.1
  417.6 118.7 all-reduce.1
